TPU v7x, 512 devices: a whole 4x8x8 slice. The times are simulated.
512 devices in a mesh: row: 16 (over y, core), col: 32 (over z, x).
Axes of the slice: x: 4, y: 8, z: 8, core: 2. Of those that a mesh axis runs over, the one named last changes fastest.
Arguments:
- grad_out: bfloat16 [2048, 8192], P('col', 'row'), may hold values from -0.09375 to 0.09375
- activations: bfloat16 [2048, 28672], P('row', 'col'), may hold values from -6 to 6
- left_steps: float32 [10, 8192], P(None, 'row')
- left_curves: float32 [10, 8192], P(None, 'row'), as said below
- right_steps: float32 [10, 28672], P(None, 'col')
- right_curves: float32 [10, 28672], P(None, 'col'), as said below
Outputs:
- direction: float32 [8192, 28672], P('row', 'col')
Inputs may be any that keep to these rules, and one draw needn't show every extreme that they name: `left_curves`: each curve row is its step row scaled entrywise by positive factors, so every step has a positive inner product with its curve; the last pair is the newest. `right_curves`: as for the output side.
All inputs are finite; a program needn't handle non-finite values.
Results may differ from a plain program's by a relative error of at most 0.0003.
Values may be sent and summed in bfloat16 or wider, within the bound.
No kernel may reach another device: no remote copies, remote signals or barrier semaphores. Data moves between devices by JAX's collectives and lax.ppermute only.
A program may use at most 64 MiB of HBM per device.

v0:
```python
import jax
import jax.numpy as jnp
from jax import lax
from jax.sharding import PartitionSpec as P

HIGH = lax.Precision.HIGHEST


def upper_inverse(upper_tri):
    count = upper_tri.shape[0]
    identity = jnp.eye(count, dtype=upper_tri.dtype)
    inv_rows = [None] * count
    for index in reversed(range(count)):
        running = identity[index]
        for later in range(index + 1, count):
            running = running - upper_tri[index, later] * inv_rows[later]
        inv_rows[index] = running / upper_tri[index, index]
    return jnp.stack(inv_rows, 0)


def compact(pair_sy, pair_yy):
    scaling = pair_sy[-1, -1] / pair_yy[-1, -1]
    upper_tri = jnp.triu(pair_sy)
    inverse = upper_inverse(upper_tri)
    middle = jnp.diag(jnp.diag(pair_sy)) + scaling * pair_yy
    return (scaling, inverse, middle)


def pair_products(step_rows, curv_rows):
    pair_sy = jnp.dot(step_rows, curv_rows.T, precision=HIGH, preferred_element_type=jnp.float32)
    pair_yy = jnp.dot(curv_rows, curv_rows.T, precision=HIGH, preferred_element_type=jnp.float32)
    return (pair_sy, pair_yy)


def apply_left(grad_block, step_rows, curv_rows, terms, proj_steps, proj_curves):
    scaling, inverse, middle = terms
    weighted = jnp.dot(inverse, proj_steps, precision=HIGH)
    coeffs = jnp.dot(
        inverse.T, jnp.dot(middle, weighted, precision=HIGH) - scaling * proj_curves, precision=HIGH
    )
    lefted = (
        scaling * grad_block
        + jnp.dot(step_rows.T, coeffs, precision=HIGH)
        - scaling * jnp.dot(curv_rows.T, weighted, precision=HIGH)
    )
    return (lefted, weighted, coeffs)


def apply_right(lefted, step_rows, curv_rows, terms, side_steps, side_curves):
    scaling, inverse, middle = terms
    weighted = jnp.dot(side_steps, inverse.T, precision=HIGH)
    coeffs = jnp.dot(
        jnp.dot(weighted, middle, precision=HIGH) - scaling * side_curves, inverse, precision=HIGH
    )
    return (
        scaling * lefted
        + jnp.dot(coeffs, step_rows, precision=HIGH)
        - scaling * jnp.dot(weighted, curv_rows, precision=HIGH)
    )


def on_device(grad_out, activations, left_steps, left_curves, right_steps, right_curves):
    contract = (((0,), (0,)), ((), ()))
    left_sy, left_yy = pair_products(left_steps, left_curves)
    right_sy, right_yy = pair_products(right_steps, right_curves)
    token_panel = lax.all_gather(activations, "row", axis=0, tiled=True)
    grad_block = lax.dot_general(
        lax.all_gather(grad_out, "col", axis=0, tiled=True),
        token_panel,
        contract,
        preferred_element_type=jnp.float32,
    )
    left_sy, left_yy = lax.psum((left_sy, left_yy), "row")
    right_sy, right_yy = lax.psum((right_sy, right_yy), "col")
    proj_steps, proj_curves = lax.psum(
        (
            jnp.dot(left_steps, grad_block, precision=HIGH),
            jnp.dot(left_curves, grad_block, precision=HIGH),
        ),
        "row",
    )
    lefted = apply_left(
        grad_block, left_steps, left_curves, compact(left_sy, left_yy), proj_steps, proj_curves
    )[0]
    side_steps, side_curves = lax.psum(
        (
            jnp.dot(lefted, right_steps.T, precision=HIGH),
            jnp.dot(lefted, right_curves.T, precision=HIGH),
        ),
        "col",
    )
    return apply_right(
        lefted, right_steps, right_curves, compact(right_sy, right_yy), side_steps, side_curves
    )


def solution(mesh):
    in_specs = (
        P("col", "row"),
        P("row", "col"),
        P(None, "row"),
        P(None, "row"),
        P(None, "col"),
        P(None, "col"),
    )
    out_specs = P("row", "col")
    return jax.shard_map(
        on_device, mesh=mesh, in_specs=in_specs, out_specs=out_specs, check_vma=False
    )
```

profile of v0, /device:TPU:8, one launch (start us, length us, event | category | flops | bytes accessed | tf_op | source)
XLA Modules:
  0.0 520.0 jit_solution(11072346568217692992)
XLA Ops:
  6.5 0.0 copy-start
  6.5 0.0 all-gather.3.cloned.1.call-start
  6.5 0.7 all-gather.3.cloned.1.call-update
  7.3 0.0 all-gather.5.cloned.1.call-start
  7.3 0.7 all-gather.5.cloned.1.call-update
  8.0 0.0 all-reduce.4.cloned.1.call-start
  8.1 1.6 fusion.26
  9.7 1.5 fusion.25
  11.2 0.0 copy-done
  11.2 0.2 fusion.24
  11.4 1.0 fusion.23
  12.4 0.0 copy-start.2
  12.5 86.7 %all-gather.3.cloned.1.call-done = bf16[2048,512]{1,0:T(8,128)(2,1)} async-done(((bf16[64,512]{1,0:T(8,128)(2,1)}), bf16[2048,512]{1,0:T(8,128)(2,1)}) %all-gather.3.cloned.1.call-update) | async-done | bytes 2097168 | tf_op jit(solution)/shard_map/all_gather | solution.py:68
  99.1 42.5 %all-gather.5.cloned.1.call-done = bf16[2048,896]{1,0:T(8,128)(2,1)} async-done(((bf16[128,896]{1,0:T(8,128)(2,1)}), bf16[2048,896]{1,0:T(8,128)(2,1)}) %all-gather.5.cloned.1.call-update) | async-done | bytes 3670032 | tf_op jit(solution)/shard_map/all_gather | solution.py:66
  141.6 5.0 fusion.27
  146.6 0.0 copy-done.2
  146.7 0.0 copy-start.1
  146.7 0.0 copy-start.4
  146.7 1.7 convolution_bitcast_fusion.1
  148.4 0.0 copy-done.1
  148.4 0.0 copy-done.4
  148.4 3.8 convolution_bitcast_fusion
  152.2 0.0 all-reduce.4.cloned.1.call-update
  152.2 112.5 %all-reduce.4.cloned.1.call-done = (f32[10,10]{1,0:T(8,128)}, f32[10,896]{0,1:T(8,128)}, f32[10,896]{1,0:T(8,128)}, f32[10,10]{1,0:T(8,128)}) async-done(((f32[10,10]{1,0:T(8,128)}, f32[10,896]{0,1:T(8,128)}, f32[10,896]{1,0:T(8,128)}, f32[10,10]{1,0:T(8,128)}), (f32[10,10]{1,0:T(8,128)}, f32[10,896]{0,1:T(8,128)}, f32[10,896]{1,0:T(8,128)}, f32[10,10]{1,0:T(8,128)})) %all-reduce.4.cloned.1.call-update) | async-done | bytes 72496 | tf_op jit(solution)/shard_map/psum | solution.py:73
  264.7 1.3 slice.532
  266.0 0.8 fusion.7
  266.8 0.7 fusion.22
  267.5 0.7 fusion.21
  268.2 0.7 fusion.20
  269.0 1.3 slice.533
  270.3 1.4 gather_fusion
  273.1 34.2 %subtract_divide_fusion.9 = (f32[1,10]{1,0:T(1,128)S(1)}, f32[1,10]{1,0:T(1,128)S(1)}, f32[1,10]{1,0:T(1,128)S(1)}, f32[1,10]{1,0:T(1,128)S(1)}, f32[1,10]{1,0:T...) fusion(f32[10,10]{1,0:T(8,128)S(1)} %fusion.8, ...), kind=kLoop, calls=%fused_computation.36 | loop fusion | flops 1000 | bytes 1020 | tf_op jit(solution)/shard_map/div | solution.py:17
  307.3 1.5 fusion.28
  308.9 1.1 convolution_subtract_fusion.1
  310.0 0.2 fusion.29
  310.2 1.6 fusion.30
  311.9 3.2 bitcast_subtract_fusion
  315.1 0.0 copy-start.3
  315.1 1.6 fusion.33
  316.7 0.0 copy-done.3
  316.7 1.8 fusion.31
  318.5 149.2 %all-reduce = (f32[512,10]{1,0:T(8,128)S(1)}, f32[10,10]{1,0:T(8,128)S(1)}, f32[512,10]{1,0:T(8,128)S(1)}, f32[10,10]{1,0:T(8,128)S(1)}) all-reduce(f32[512,10]{1,0:T(8,128)S(1)} %fusion.31, f32[10,10]{1,0:T(8,128)S(1)} %fusion.23, f32[512,10]{1,0:T(8,128)S(1)} %fusion.33, ...), channel_id=1, replica_groups=mesh['row'=16,'col'=32] {'col'}, use_global_device_ids=true, to_apply=%region_6.7 | all-reduce | flops 10440 | bytes 83520 | tf_op jit(solution)/shard_map/psum | solution.py:85
  467.7 0.6 slice.530
  468.3 0.7 gather_fusion.1
  469.0 0.1 fusion.6
  469.1 0.7 fusion.19
  469.8 0.7 fusion.18
  470.5 0.7 fusion.17
  471.3 0.6 slice.531
  473.2 34.4 %subtract_divide_fusion = (f32[1,10]{1,0:T(1,128)S(1)}, f32[1,10]{1,0:T(1,128)S(1)}, f32[1,10]{1,0:T(1,128)S(1)}, f32[1,10]{1,0:T(1,128)S(1)}, f32[1,10]{1,0:T(1...) fusion(f32[10,10]{1,0:T(8,128)S(1)} %fusion.8, ...), kind=kLoop, calls=%fused_computation.27 | loop fusion | flops 1000 | bytes 1020 | tf_op jit(solution)/shard_map/div | solution.py:17
  507.6 0.3 fusion.32
  507.9 0.6 convolution_subtract_fusion
  508.6 0.3 fusion.34
  508.9 1.6 fusion.35
  510.5 3.0 multiply_subtract_fusion
  (5 shorter events, 0.1 us)
Async XLA Ops:
  6.5 4.7 copy-start
  6.5 92.6 %all-gather.3.cloned.1.call-start = ((), (), s32[]{:S(2)}) async-start(), calls=%async_computation | async-start | bytes 2162688 | tf_op jit(solution)/shard_map/all_gather | solution.py:68
  7.3 134.4 %all-gather.5.cloned.1.call-start = ((), (), s32[]{:S(2)}) async-start(), calls=%async_computation.1 | async-start | bytes 3899392 | tf_op jit(solution)/shard_map/all_gather | solution.py:66
  8.0 256.7 %all-reduce.4.cloned.1.call-start = ((), (), s32[]{:S(2)}) async-start(), calls=%async_computation.2 | async-start | bytes 1064960 | tf_op jit(solution)/shard_map/psum | solution.py:73
  12.4 134.2 %copy-start.2 = (f32[10,512]{1,0:T(8,128)S(1)}, f32[10,512]{1,0:T(8,128)}, u32[]{:S(2)}) copy-start(f32[10,512]{1,0:T(8,128)} %param.9) | copy-start | bytes 61444
  146.7 1.7 copy-start.1
  146.7 1.7 copy-start.4
  315.1 1.6 copy-start.3
Sparse Core Ops, SparseCore 0:
  10.5 88.6 all-gather.2
  101.3 40.3 all-gather.4
  152.3 112.3 all-reduce.3
where the time goes:
time: 522 us; the launch traced here: 520 us
  waiting for transfers between devices  243 us (47%)
  blocking collectives  149 us (29%)
  other arithmetic  69.5 us (13%)
  matrix products  31.9 us (6%)
  between operations  15.9 us (3%)
  local copies, waits for them, and re-layouts  10.4 us (2%)
    psum x1, blocking collectives, on_device(): lax.psum((jnp.dot(lefted, right_steps.T, precision=HIGH), jnp.dot(lefted,...  149 us
    psum x1, waiting for transfers between devices, on_device(): left_sy, left_yy = lax.psum((left_sy, left_yy), 'row')  113 us
    all_gather x1, waiting for transfers between devices, on_device(): lax.all_gather(grad_out, 'col', axis=0, tiled=True)  86.7 us
    div x2, other arithmetic, upper_inverse(): inv_rows[index] = running / upper_tri[index, index]  68.6 us
    all_gather x1, waiting for transfers between devices, on_device(): token_panel = lax.all_gather(activations, 'row', axis=0, tiled=True)  42.5 us
  transfers between devices with their start and end apart: 3, of which 3 were waited for; matrix products, arithmetic and copies ran while one was open for 1% of the time, Pallas kernels for 0%

commit v1 on v0

--- a/solution.py
+++ b/solution.py
@@ -1,9 +1,37 @@
+import functools
 import jax
 import jax.numpy as jnp
 from jax import lax
 from jax.sharding import PartitionSpec as P
+from jax.lax import axis_index, ppermute, psum
 
 HIGH = lax.Precision.HIGHEST
+
+
+def draw_digits_in(mine_x, across, dim_no):
+    state_now, z, block_now = (psum(1, across), axis_index(across), mine_x.shape[dim_no])
+    by_rank = [(src_i, (src_i + 1) % state_now) for src_i in range(state_now)]
+    state_next = jnp.zeros(
+        (*mine_x.shape[:dim_no], state_now * block_now, *mine_x.shape[dim_no + 1 :]), mine_x.dtype
+    )
+    runs = [(src_i, (src_i - 1) % state_now) for src_i in range(state_now)]
+    ready = v_now = mine_x
+    state_next = lax.dynamic_update_slice_in_dim(state_next, mine_x, z * block_now, axis=dim_no)
+    after = state_now // 2
+    for pp in tuple(range(1, after + 1)):
+        ready = ppermute(ready, across, by_rank)
+        state_next = lax.dynamic_update_slice_in_dim(
+            state_next, ready, (z - pp) % state_now * block_now, axis=dim_no
+        )
+        if pp < state_now - after:
+            v_now = ppermute(v_now, across, runs)
+            state_next = lax.dynamic_update_slice_in_dim(
+                state_next, v_now, (z + pp) % state_now * block_now, axis=dim_no
+            )
+    return state_next
+
+
+mark_results = functools.partial(draw_digits_in, across="row", dim_no=0)
 
 
 def upper_inverse(upper_tri):
@@ -63,7 +91,7 @@
     contract = (((0,), (0,)), ((), ()))
     left_sy, left_yy = pair_products(left_steps, left_curves)
     right_sy, right_yy = pair_products(right_steps, right_curves)
-    token_panel = lax.all_gather(activations, "row", axis=0, tiled=True)
+    token_panel = mark_results(activations)
     grad_block = lax.dot_general(
         lax.all_gather(grad_out, "col", axis=0, tiled=True),
         token_panel,

time: 522 us -> 480 us (0.920)
  waiting for transfers between devices: 243 us -> 169 us
  starting transfers between devices: 0.08 us -> 18.7 us
  local copies, waits for them, and re-layouts: 10.4 us -> 26.5 us
    all_gather x1, waiting for transfers between devices: 86.7 us -> 38.6 us  [on_device(): lax.all_gather(grad_out, 'col', axis=0, tiled=True)]
    all_gather x1 -> x0, waiting for transfers between devices: 42.5 us -> none  [on_device(): token_panel = lax.all_gather(activations, 'row', axis=0, tiled=True)]
    ppermute x0 -> x15, waiting for transfers between devices: none -> 19.2 us  [the longest x8 19.2 us: draw_digits_in(): ready = ppermute(ready, across, by_rank)]
    ppermute x0 -> x15, starting transfers between devices: none -> 18.6 us  [the longest x7 18.6 us: draw_digits_in(): v_now = ppermute(v_now, across, runs)]
    dynamic_update_slice x0 -> x16, local copies, waits for them, and re-layouts: none -> 11.3 us  [the longest x8 5.66 us: draw_digits_in(): lax.dynamic_update_slice_in_dim(state_next, ready, (z - pp) % state_now *...]
  transfers between devices with their start and end apart: 3 -> 17, of which waited for: 3 -> 9; matrix products, arithmetic and copies ran while one was open for 1% -> 3% of each run, Pallas kernels for 0% -> 0%
where the time goes in v1:
time: 480 us; the launch traced here: 479 us
  waiting for transfers between devices  169 us (35%)
  blocking collectives  149 us (31%)
  other arithmetic  69.5 us (14%)
  matrix products  30.2 us (6%)
  local copies, waits for them, and re-layouts  26.5 us (6%)
  starting transfers between devices  18.7 us (4%)
  between operations  16.4 us (3%)
    psum x1, blocking collectives, on_device(): lax.psum((jnp.dot(lefted, right_steps.T, precision=HIGH), jnp.dot(lefted,...  149 us
    psum x1, waiting for transfers between devices, on_device(): left_sy, left_yy = lax.psum((left_sy, left_yy), 'row')  110 us
    div x2, other arithmetic, upper_inverse(): inv_rows[index] = running / upper_tri[index, index]  68.6 us
    all_gather x1, waiting for transfers between devices, on_device(): lax.all_gather(grad_out, 'col', axis=0, tiled=True)  38.6 us
    ppermute x8, waiting for transfers between devices, draw_digits_in(): ready = ppermute(ready, across, by_rank)  19.2 us
    ppermute x7, starting transfers between devices, draw_digits_in(): v_now = ppermute(v_now, across, runs)  18.6 us
  transfers between devices with their start and end apart: 17, of which 9 were waited for; matrix products, arithmetic and copies ran while one was open for 3% of the time, Pallas kernels for 0%

profile of v1, /device:TPU:8, one launch (start us, length us, event | category | flops | bytes accessed | tf_op | source)
XLA Modules:
  0.0 479.1 jit_solution(6231306002654439550)
XLA Ops:
  6.6 0.7 all-gather.2.cloned.1.call-update
  7.4 1.7 collective-permute-start.1
  9.1 2.0 broadcast_in_dim.39
  11.2 0.7 constant_dynamic-update-slice_fusion.15
  11.9 0.8 fusion.27
  12.6 0.8 fusion.26
  14.0 4.2 collective-permute-start.3
  18.2 0.7 constant_dynamic-update-slice_fusion.14
  18.9 0.7 constant_dynamic-update-slice_fusion.13
  19.6 2.3 collective-permute-done.2
  21.8 1.8 collective-permute-start.5
  23.6 0.7 constant_dynamic-update-slice_fusion.12
  24.3 0.7 constant_dynamic-update-slice_fusion.11
  25.0 2.3 collective-permute-done.4
  27.3 1.9 collective-permute-start.7
  29.2 0.7 constant_dynamic-update-slice_fusion.10
  29.9 0.7 constant_dynamic-update-slice_fusion.9
  30.6 2.3 collective-permute-done.6
  32.8 3.0 collective-permute-start.9
  35.8 0.7 constant_dynamic-update-slice_fusion.8
  36.5 0.7 constant_dynamic-update-slice_fusion.7
  37.2 2.3 collective-permute-done.8
  39.5 3.0 collective-permute-start.11
  42.5 0.7 constant_dynamic-update-slice_fusion.6
  43.2 0.7 constant_dynamic-update-slice_fusion.5
  43.9 2.3 collective-permute-done.10
  46.1 3.1 collective-permute-start.13
  49.2 0.7 constant_dynamic-update-slice_fusion.4
  49.9 0.7 constant_dynamic-update-slice_fusion.3
  50.6 2.3 collective-permute-done.12
  52.9 0.7 constant_dynamic-update-slice_fusion.2
  53.6 0.7 constant_dynamic-update-slice_fusion.1
  54.3 5.6 %collective-permute-done.14 = bf16[128,896]{1,0:T(8,128)(2,1)S(1)} collective-permute-done((bf16[128,896]{1,0:T(8,128)(2,1)S(1)}, bf16[128,896]{1,0:T(8,128)(2,1)S(1)}, u32[]{:S(2)}, u32[]{:S(2)}) %collective-permute-start.14) | collective-permute-done | bytes 229408 | tf_op jit(solution)/shard_map/ppermute | solution.py:22
  59.9 0.7 constant_dynamic-update-slice_fusion
  60.6 38.6 %all-gather.2.cloned.1.call-done = bf16[2048,512]{1,0:T(8,128)(2,1)} async-done(((bf16[64,512]{1,0:T(8,128)(2,1)}), bf16[2048,512]{1,0:T(8,128)(2,1)}) %all-gather.2.cloned.1.call-update) | async-done | bytes 2097168 | tf_op jit(solution)/shard_map/all_gather | solution.py:96
  99.2 4.8 fusion.28
  104.0 2.3 convolution_bitcast_fusion
  106.3 2.3 convolution_bitcast_fusion.1
  108.6 110.0 %all-reduce.4.cloned.1.call-done = (f32[10,10]{1,0:T(8,128)}, f32[10,896]{0,1:T(8,128)}, f32[10,896]{1,0:T(8,128)}, f32[10,10]{1,0:T(8,128)}) async-done(((f32[10,10]{1,0:T(8,128)}, f32[10,896]{0,1:T(8,128)}, f32[10,896]{1,0:T(8,128)}, f32[10,10]{1,0:T(8,128)}), (f32[10,10]{1,0:T(8,128)}, f32[10,896]{0,1:T(8,128)}, f32[10,896]{1,0:T(8,128)}, f32[10,10]{1,0:T(8,128)})) %all-reduce.4.cloned.1.call-update) | async-done | bytes 72496 | tf_op jit(solution)/shard_map/psum | solution.py:101
  218.7 1.3 slice.532
  220.0 0.8 fusion.8
  220.7 0.7 fusion.22
  221.5 0.7 fusion.21
  222.2 0.7 fusion.23
  222.9 1.3 slice.533
  224.2 1.4 gather_fusion
  226.9 34.4 %subtract_divide_fusion.9 = (f32[1,10]{1,0:T(1,128)S(1)}, f32[1,10]{1,0:T(1,128)S(1)}, f32[1,10]{1,0:T(1,128)S(1)}, f32[1,10]{1,0:T(1,128)S(1)}, f32[1,10]{1,0:T...) fusion(f32[10,10]{1,0:T(8,128)S(1)} %fusion.9, ...), kind=kLoop, calls=%fused_computation.52 | loop fusion | flops 1000 | bytes 1020 | tf_op jit(solution)/shard_map/div | solution.py:45
  261.4 1.5 fusion.29
  262.9 1.1 convolution_subtract_fusion.1
  264.3 1.6 fusion.31
  265.9 1.9 multiply_subtract_fusion
  267.8 3.3 fusion.32
  271.1 3.1 fusion.34
  274.2 149.3 %all-reduce = (f32[512,10]{1,0:T(8,128)S(1)}, f32[10,10]{1,0:T(8,128)S(1)}, f32[512,10]{1,0:T(8,128)S(1)}, f32[10,10]{1,0:T(8,128)S(1)}) all-reduce(f32[512,10]{1,0:T(8,128)S(1)} %fusion.32, f32[10,10]{1,0:T(8,128)S(1)} %fusion.24, f32[512,10]{1,0:T(8,128)S(1)} %fusion.34, ...), channel_id=1, replica_groups=mesh['row'=16,'col'=32] {'col'}, use_global_device_ids=true, to_apply=%region_6.7 | all-reduce | flops 10440 | bytes 83520 | tf_op jit(solution)/shard_map/psum | solution.py:113
  423.6 0.7 slice.530
  424.3 0.7 fusion.18
  425.0 0.7 fusion.19
  425.7 0.7 fusion.20
  426.4 0.7 gather_fusion.1
  427.1 0.7 slice.531
  429.2 34.2 %subtract_divide_fusion = (f32[1,10]{1,0:T(1,128)S(1)}, f32[1,10]{1,0:T(1,128)S(1)}, f32[1,10]{1,0:T(1,128)S(1)}, f32[1,10]{1,0:T(1,128)S(1)}, f32[1,10]{1,0:T(1...) fusion(f32[10,10]{1,0:T(8,128)S(1)} %fusion.9, ...), kind=kLoop, calls=%fused_computation.43 | loop fusion | flops 1000 | bytes 1020 | tf_op jit(solution)/shard_map/div | solution.py:45
  464.8 1.6 fusion.36
  466.4 3.1 fusion
  469.5 2.7 copy.12
  (45 shorter events, 2.3 us)
Async XLA Ops:
  6.5 6.9 %copy-start = (f32[10,896]{1,0:T(8,128)S(1)}, f32[10,896]{1,0:T(8,128)}, u32[]{:S(2)}) copy-start(f32[10,896]{1,0:T(8,128)} %param.11) | copy-start | bytes 107524
  6.5 4.6 copy-start.6
  6.5 5.3 %copy-start.3 = (f32[10,512]{1,0:T(8,128)S(1)}, f32[10,512]{1,0:T(8,128)}, u32[]{:S(2)}) copy-start(f32[10,512]{1,0:T(8,128)} %param.9) | copy-start | bytes 61444
  6.5 6.1 %copy-start.5 = (f32[10,512]{1,0:T(8,128)S(1)}, f32[10,512]{1,0:T(8,128)}, u32[]{:S(2)}) copy-start(f32[10,512]{1,0:T(8,128)} %param.8) | copy-start | bytes 61444
  6.5 7.2 %copy-start.4 = (f32[10,896]{1,0:T(8,128)S(1)}, f32[10,896]{1,0:T(8,128)}, u32[]{:S(2)}) copy-start(f32[10,896]{1,0:T(8,128)} %param.10) | copy-start | bytes 107524
  6.5 92.7 %all-gather.2.cloned.1.call-start = ((), (), s32[]{:S(2)}) async-start(), calls=%async_computation | async-start | bytes 2162688 | tf_op jit(solution)/shard_map/all_gather | solution.py:96
  7.3 211.4 %all-reduce.4.cloned.1.call-start = ((), (), s32[]{:S(2)}) async-start(), calls=%async_computation.1 | async-start | bytes 1064960 | tf_op jit(solution)/shard_map/psum | solution.py:101
  7.3 6.6 %collective-permute-start = (bf16[128,896]{1,0:T(8,128)(2,1)}, bf16[128,896]{1,0:T(8,128)(2,1)S(1)}, u32[]{:S(2)}, u32[]{:S(2)}) collective-permute-start(bf16[128,896]{1,0:T(8,128)(2,1)} %param.7), channel_id=1, source_target_pairs={{0,32},{32,64},{64,96},{96,128},{128,160},{160,192},{192,224},{224... | collective-permute-start | bytes 688136 | tf_op jit(solution)/shard_map/ppermute | solution.py:22
  7.4 6.6 %collective-permute-start.1 = (bf16[128,896]{1,0:T(8,128)(2,1)}, bf16[128,896]{1,0:T(8,128)(2,1)S(1)}, u32[]{:S(2)}, u32[]{:S(2)}) collective-permute-start(bf16[128,896]{1,0:T(8,128)(2,1)} %param.7), channel_id=1, source_target_pairs={{0,480},{32,0},{64,32},{96,64},{128,96},{160,128},{192,160},{224,1... | collective-permute-start | bytes 688136 | tf_op jit(solution)/shard_map/ppermute | solution.py:27
  13.9 7.9 %collective-permute-start.2 = (bf16[128,896]{1,0:T(8,128)(2,1)S(1)}, bf16[128,896]{1,0:T(8,128)(2,1)S(1)}, u32[]{:S(2)}, u32[]{:S(2)}) collective-permute-start(bf16[128,896]{1,0:T(8,128)(2,1)S(1)} %collective-permute-done), channel_id=1, source_target_pairs={{0,32},{32,64},{64,96},{96,128},{128,160},{160,192},{192,224},{224... | collective-permute-start | bytes 688136 | tf_op jit(solution)/shard_map/ppermute | solution.py:22
  14.0 7.9 %collective-permute-start.3 = (bf16[128,896]{1,0:T(8,128)(2,1)S(1)}, bf16[128,896]{1,0:T(8,128)(2,1)S(1)}, u32[]{:S(2)}, u32[]{:S(2)}) collective-permute-start(bf16[128,896]{1,0:T(8,128)(2,1)S(1)} %collective-permute-done.1), channel_id=1, source_target_pairs={{0,480},{32,0},{64,32},{96,64},{128,96},{160,128},{192,160},{224,1... | collective-permute-start | bytes 688136 | tf_op jit(solution)/shard_map/ppermute | solution.py:27
  21.8 5.4 %collective-permute-start.4 = (bf16[128,896]{1,0:T(8,128)(2,1)S(1)}, bf16[128,896]{1,0:T(8,128)(2,1)S(1)}, u32[]{:S(2)}, u32[]{:S(2)}) collective-permute-start(bf16[128,896]{1,0:T(8,128)(2,1)S(1)} %collective-permute-done.2), channel_id=1, source_target_pairs={{0,32},{32,64},{64,96},{96,128},{128,160},{160,192},{192,224},{224... | collective-permute-start | bytes 688136 | tf_op jit(solution)/shard_map/ppermute | solution.py:22
  21.8 5.4 %collective-permute-start.5 = (bf16[128,896]{1,0:T(8,128)(2,1)S(1)}, bf16[128,896]{1,0:T(8,128)(2,1)S(1)}, u32[]{:S(2)}, u32[]{:S(2)}) collective-permute-start(bf16[128,896]{1,0:T(8,128)(2,1)S(1)} %collective-permute-done.3), channel_id=1, source_target_pairs={{0,480},{32,0},{64,32},{96,64},{128,96},{160,128},{192,160},{224,1... | collective-permute-start | bytes 688136 | tf_op jit(solution)/shard_map/ppermute | solution.py:27
  27.3 5.6 %collective-permute-start.6 = (bf16[128,896]{1,0:T(8,128)(2,1)S(1)}, bf16[128,896]{1,0:T(8,128)(2,1)S(1)}, u32[]{:S(2)}, u32[]{:S(2)}) collective-permute-start(bf16[128,896]{1,0:T(8,128)(2,1)S(1)} %collective-permute-done.4), channel_id=1, source_target_pairs={{0,32},{32,64},{64,96},{96,128},{128,160},{160,192},{192,224},{224... | collective-permute-start | bytes 688136 | tf_op jit(solution)/shard_map/ppermute | solution.py:22
  27.3 5.6 %collective-permute-start.7 = (bf16[128,896]{1,0:T(8,128)(2,1)S(1)}, bf16[128,896]{1,0:T(8,128)(2,1)S(1)}, u32[]{:S(2)}, u32[]{:S(2)}) collective-permute-start(bf16[128,896]{1,0:T(8,128)(2,1)S(1)} %collective-permute-done.5), channel_id=1, source_target_pairs={{0,480},{32,0},{64,32},{96,64},{128,96},{160,128},{192,160},{224,1... | collective-permute-start | bytes 688136 | tf_op jit(solution)/shard_map/ppermute | solution.py:27
  32.8 6.6 %collective-permute-start.8 = (bf16[128,896]{1,0:T(8,128)(2,1)S(1)}, bf16[128,896]{1,0:T(8,128)(2,1)S(1)}, u32[]{:S(2)}, u32[]{:S(2)}) collective-permute-start(bf16[128,896]{1,0:T(8,128)(2,1)S(1)} %collective-permute-done.6), channel_id=1, source_target_pairs={{0,32},{32,64},{64,96},{96,128},{128,160},{160,192},{192,224},{224... | collective-permute-start | bytes 688136 | tf_op jit(solution)/shard_map/ppermute | solution.py:22
  32.8 6.6 %collective-permute-start.9 = (bf16[128,896]{1,0:T(8,128)(2,1)S(1)}, bf16[128,896]{1,0:T(8,128)(2,1)S(1)}, u32[]{:S(2)}, u32[]{:S(2)}) collective-permute-start(bf16[128,896]{1,0:T(8,128)(2,1)S(1)} %collective-permute-done.7), channel_id=1, source_target_pairs={{0,480},{32,0},{64,32},{96,64},{128,96},{160,128},{192,160},{224,1... | collective-permute-start | bytes 688136 | tf_op jit(solution)/shard_map/ppermute | solution.py:27
  39.5 6.7 %collective-permute-start.10 = (bf16[128,896]{1,0:T(8,128)(2,1)S(1)}, bf16[128,896]{1,0:T(8,128)(2,1)S(1)}, u32[]{:S(2)}, u32[]{:S(2)}) collective-permute-start(bf16[128,896]{1,0:T(8,128)(2,1)S(1)} %collective-permute-done.8), channel_id=1, source_target_pairs={{0,32},{32,64},{64,96},{96,128},{128,160},{160,192},{192,224},{224... | collective-permute-start | bytes 688136 | tf_op jit(solution)/shard_map/ppermute | solution.py:22
  39.5 6.7 %collective-permute-start.11 = (bf16[128,896]{1,0:T(8,128)(2,1)S(1)}, bf16[128,896]{1,0:T(8,128)(2,1)S(1)}, u32[]{:S(2)}, u32[]{:S(2)}) collective-permute-start(bf16[128,896]{1,0:T(8,128)(2,1)S(1)} %collective-permute-done.9), channel_id=1, source_target_pairs={{0,480},{32,0},{64,32},{96,64},{128,96},{160,128},{192,160},{224,1... | collective-permute-start | bytes 688136 | tf_op jit(solution)/shard_map/ppermute | solution.py:27
  46.1 6.8 %collective-permute-start.12 = (bf16[128,896]{1,0:T(8,128)(2,1)S(1)}, bf16[128,896]{1,0:T(8,128)(2,1)S(1)}, u32[]{:S(2)}, u32[]{:S(2)}) collective-permute-start(bf16[128,896]{1,0:T(8,128)(2,1)S(1)} %collective-permute-done.10), channel_id=1, source_target_pairs={{0,32},{32,64},{64,96},{96,128},{128,160},{160,192},{192,224},{224... | collective-permute-start | bytes 688136 | tf_op jit(solution)/shard_map/ppermute | solution.py:22
  46.1 7.5 %collective-permute-start.13 = (bf16[128,896]{1,0:T(8,128)(2,1)S(1)}, bf16[128,896]{1,0:T(8,128)(2,1)S(1)}, u32[]{:S(2)}, u32[]{:S(2)}) collective-permute-start(bf16[128,896]{1,0:T(8,128)(2,1)S(1)} %collective-permute-done.11), channel_id=1, source_target_pairs={{0,480},{32,0},{64,32},{96,64},{128,96},{160,128},{192,160},{224,1... | collective-permute-start | bytes 688136 | tf_op jit(solution)/shard_map/ppermute | solution.py:27
  52.9 7.0 %collective-permute-start.14 = (bf16[128,896]{1,0:T(8,128)(2,1)S(1)}, bf16[128,896]{1,0:T(8,128)(2,1)S(1)}, u32[]{:S(2)}, u32[]{:S(2)}) collective-permute-start(bf16[128,896]{1,0:T(8,128)(2,1)S(1)} %collective-permute-done.12), channel_id=1, source_target_pairs={{0,32},{32,64},{64,96},{96,128},{128,160},{160,192},{192,224},{224... | collective-permute-start | bytes 688136 | tf_op jit(solution)/shard_map/ppermute | solution.py:22
  267.8 3.3 copy-start.1
  274.2 192.2 %copy-start.2 = (f32[896,512]{1,0:T(8,128)S(1)}, f32[896,512]{1,0:T(8,128)}, u32[]{:S(2)}) copy-start(f32[896,512]{1,0:T(8,128)} %copy-done.1) | copy-start | bytes 5505028
Sparse Core Ops, SparseCore 0:
  10.5 88.6 all-gather.1
  108.7 109.8 all-reduce.3
